TPU v7x, 128 devices: a whole 4x4x4 slice. The times are simulated.
128 devices in a mesh: leaf: 16 (over x, y), side: 8 (over z, core).
Axes of the slice: x: 4, y: 4, z: 4, core: 2. Of those that a mesh axis runs over, the one named last changes fastest.
Arguments:
- block: float32 [131072, 512], P(('leaf', 'side')), may hold values from -24 to 24
- basis: float32 [131072, 1024], P(('leaf', 'side')), may hold values from -1 to 1
Outputs:
- ortho: float32 [131072, 512], P(('leaf', 'side'))
- factor: float32 [512, 512], replicated
- coeffs: float32 [1024, 512], replicated
All inputs are finite; a program needn't handle non-finite values.
Results may differ from a plain program's by a relative error of at most 0.0001.
Values sent between devices are 32-bit elements; how exact they have to be, the bound alone decides.
A program may use at most 64 MiB of HBM per device.

v0:
```python
import jax
import jax.numpy as jnp
from jax import lax
from jax.sharding import PartitionSpec as P


def inner(left, right):
    return lax.dot_general(
        left,
        right,
        (((0,), (0,)), ((), ())),
        precision=lax.Precision.HIGHEST,
        preferred_element_type=jnp.float32,
    )


def product(left, right):
    return jnp.dot(left, right, precision=lax.Precision.HIGHEST, preferred_element_type=jnp.float32)


def small_upper(matrix):
    width = matrix.shape[0]
    positions = jnp.arange(width, dtype=jnp.int32)

    def one_step(column, carry):
        rest, result = carry
        column = jnp.asarray(column).astype(jnp.int32)
        row = lax.dynamic_slice_in_dim(rest, column, 1, 0)[0]
        pivot = jnp.sqrt(jnp.sum(jnp.where(positions == column, row, jnp.float32(0.0))))
        new_row = jnp.where(positions >= column, row / pivot, jnp.float32(0.0))
        result = lax.dynamic_update_slice_in_dim(result, new_row[None, :], column, 0)
        rest = rest - new_row[:, None] * new_row[None, :]
        return (rest, result)

    start = (matrix, jnp.zeros_like(matrix))
    return lax.fori_loop(0, width, one_step, start)[1]


def small_inverse(upper_block):
    width = upper_block.shape[0]
    positions = jnp.arange(width, dtype=jnp.int32)

    def one_step(count, result):
        index = (width - 1 - jnp.asarray(count)).astype(jnp.int32)
        row = lax.dynamic_slice_in_dim(upper_block, index, 1, 0)[0]
        pivot = jnp.sum(jnp.where(positions == index, row, jnp.float32(0.0)))
        beyond = jnp.where(positions > index, row, jnp.float32(0.0))
        unit = jnp.where(positions == index, jnp.float32(1.0), jnp.float32(0.0))
        new_row = (unit - product(beyond[None, :], result)[0]) / pivot
        return lax.dynamic_update_slice_in_dim(result, new_row[None, :], index, 0)

    return lax.fori_loop(0, width, one_step, jnp.zeros_like(upper_block))


def factor_and_inverse(gram):
    width = gram.shape[0]
    piece = min(128, width)
    count = width // piece
    rest = gram
    strips = []
    diag_inverses = []
    for index in range(count):
        diag = small_upper(rest[:piece, :piece])
        diag_inv = small_inverse(diag)
        right = product(diag_inv.T, rest[:piece, piece:])
        left_zeros = jnp.zeros((piece, index * piece), gram.dtype)
        strips.append(jnp.concatenate([left_zeros, diag, right], axis=1))
        diag_inverses.append(diag_inv)
        rest = rest[piece:, piece:] - inner(right, right)
    factor = jnp.concatenate(strips, axis=0)
    lower_part = None
    for index in reversed(range(count)):
        diag_inv = diag_inverses[index]
        if lower_part is None:
            lower_part = diag_inv
        else:
            coupling = factor[index * piece : (index + 1) * piece, (index + 1) * piece :]
            far = -product(diag_inv, product(coupling, lower_part))
            top = jnp.concatenate([diag_inv, far], axis=1)
            below = jnp.concatenate(
                [jnp.zeros((lower_part.shape[0], piece), gram.dtype), lower_part], axis=1
            )
            lower_part = jnp.concatenate([top, below], axis=0)
    return (factor, lower_part)


def shards(block, basis):
    rows_total = block.shape[0] * lax.axis_size("leaf") * lax.axis_size("side")
    coeffs = lax.psum(inner(basis, block), ("leaf", "side"))
    projected = block - product(basis, coeffs)
    local_gram = inner(projected, projected) / rows_total
    factor, inverse = factor_and_inverse(lax.psum(local_gram, ("leaf", "side")))
    ortho = product(projected, inverse)
    return (ortho, factor, coeffs)


def solution(mesh):
    return jax.shard_map(
        shards,
        mesh=mesh,
        in_specs=(P(("leaf", "side"), None), P(("leaf", "side"), None)),
        out_specs=(P(("leaf", "side"), None), P(), P()),
        check_vma=False,
    )
```

profile of v0, /device:TPU:1, one launch (start us, length us, event | category | flops | bytes accessed | tf_op | source)
XLA Modules:
  0.0 1886.3 jit_solution(14410040137876746820)
XLA Ops:
  7.2 10.2 fusion.74
  17.7 1.3 copy-done
  19.0 1.8 copy.5
  20.8 150.3 %all-reduce.7.cloned.1.call-done = f32[1024,512]{1,0:T(8,128)} async-done(((f32[1024,512]{1,0:T(8,128)}), f32[1024,512]{1,0:T(8,128)}) %all-reduce.7.cloned.1.call-update) | async-done | bytes 2097168 | tf_op jit(solution)/shard_map/psum | solution.py:89
  171.2 16.2 bitcast_subtract_fusion
  187.3 4.5 convolution_multiply_fusion
  191.8 145.8 %all-reduce.9.cloned.1.call-done = f32[512,512]{1,0:T(8,128)} async-done(((f32[512,512]{1,0:T(8,128)}), f32[512,512]{1,0:T(8,128)}) %all-reduce.9.cloned.1.call-update) | async-done | bytes 1048592 | tf_op jit(solution)/shard_map/psum | solution.py:92
  337.6 0.8 slice.36
  338.5 192.5 %while.136 = (s32[]{:T(128)}, f32[128,128]{1,0:T(8,128)S(1)}, f32[128,128]{1,0:T(8,128)S(1)}, s32[]{:T(128)}, s32[]{:T(128)}) while((s32[]{:T(128)}, f32[128,128]{1,0:T(8,128)S(1)}, f32[128,128]{1,0:T(8,128)S(1)}, s32[]{:T(128)}, s32[]{:T(128)}) %tuple.273), condition=%wide.region_4.5_spmd.clone.clone, body=%wide.region_2.4_spmd.clone.clone.sunk | while | flops 34305 | bytes 142421 | solution.py:36
  531.0 187.3 %while.137 = (s32[]{:T(128)}, f32[128,128]{1,0:T(8,128)S(1)}, f32[128,128]{1,0:T(8,128)S(1)}, s32[]{:T(128)}, s32[]{:T(128)}, /*index=5*/s32[]{:T(128)}, s32[]{:T(128)}) while((s32[]{:T(128)}, f32[128,128]{1,0:T(8,128)S(1)}, f32[128,128]{1,0:T(8,128)S(1)}, s32[]{:T(128)}, s32[]{:T(128)}, /*index=5*/s32[]{:T(128)}, ...), condition=%wide.region_7.8_spmd.clone.clone, body=%wide.region_5.7_spmd.clone.clone.sunk | while | flops 197765 | bytes 69783 | solution.py:52
  531.6 0.8 fusion.139
  557.9 0.8 fusion.139
  559.4 0.8 fusion.139
  585.7 0.8 fusion.139
  587.1 0.8 fusion.139
  613.4 0.8 fusion.139
  614.9 0.8 fusion.139
  641.2 0.8 fusion.139
  642.7 0.8 fusion.139
  669.0 0.8 fusion.139
  670.4 0.8 fusion.139
  696.8 0.8 fusion.139
  698.2 0.8 fusion.139
  718.9 1.3 fusion.63
  720.2 1.7 convolution_subtract_fusion
  722.0 192.5 %while.138 = (s32[]{:T(128)}, f32[128,128]{1,0:T(8,128)S(1)}, f32[128,128]{1,0:T(8,128)S(1)}, s32[]{:T(128)}, s32[]{:T(128)}) while((s32[]{:T(128)}, f32[128,128]{1,0:T(8,128)S(1)}, f32[128,128]{1,0:T(8,128)S(1)}, s32[]{:T(128)}, s32[]{:T(128)}) %tuple.279), condition=%wide.region_10.11_spmd.clone.clone, body=%wide.region_8.10_spmd.clone.clone.sunk | while | flops 34305 | bytes 142421 | solution.py:36
  914.5 187.1 %while.139 = (s32[]{:T(128)}, f32[128,128]{1,0:T(8,128)S(1)}, f32[128,128]{1,0:T(8,128)S(1)}, s32[]{:T(128)}, s32[]{:T(128)}, /*index=5*/s32[]{:T(128)}, s32[]{:T(128)}) while((s32[]{:T(128)}, f32[128,128]{1,0:T(8,128)S(1)}, f32[128,128]{1,0:T(8,128)S(1)}, s32[]{:T(128)}, s32[]{:T(128)}, /*index=5*/s32[]{:T(128)}, ...), condition=%wide.region_13.14_spmd.clone.clone, body=%wide.region_11.13_spmd.clone.clone.sunk | while | flops 197765 | bytes 69783 | solution.py:52
  918.0 0.8 fusion.145
  919.5 0.8 fusion.145
  945.8 0.8 fusion.145
  947.2 0.8 fusion.145
  973.5 0.8 fusion.145
  975.0 0.8 fusion.145
  1001.3 0.8 fusion.145
  1002.8 0.8 fusion.145
  1029.1 0.8 fusion.145
  1030.5 0.8 fusion.145
  1056.9 0.8 fusion.145
  1102.9 192.5 %while.140 = (s32[]{:T(128)}, f32[128,128]{1,0:T(8,128)S(1)}, f32[128,128]{1,0:T(8,128)S(1)}, s32[]{:T(128)}, s32[]{:T(128)}) while((s32[]{:T(128)}, f32[128,128]{1,0:T(8,128)S(1)}, f32[128,128]{1,0:T(8,128)S(1)}, s32[]{:T(128)}, s32[]{:T(128)}) %tuple.285), condition=%wide.region_16.17_spmd.clone.clone, body=%wide.region_14.16_spmd.clone.clone.sunk | while | flops 34305 | bytes 142421 | solution.py:36
  1295.4 187.1 %while.141 = (s32[]{:T(128)}, f32[128,128]{1,0:T(8,128)S(1)}, f32[128,128]{1,0:T(8,128)S(1)}, s32[]{:T(128)}, s32[]{:T(128)}, /*index=5*/s32[]{:T(128)}, s32[]{:T(128)}) while((s32[]{:T(128)}, f32[128,128]{1,0:T(8,128)S(1)}, f32[128,128]{1,0:T(8,128)S(1)}, s32[]{:T(128)}, s32[]{:T(128)}, /*index=5*/s32[]{:T(128)}, ...), condition=%wide.region_19.20_spmd.clone.clone, body=%wide.region_17.19_spmd.clone.clone.sunk | while | flops 197765 | bytes 69783 | solution.py:52
  1483.7 192.5 %while.142 = (s32[]{:T(128)}, f32[128,128]{1,0:T(8,128)S(1)}, f32[128,128]{1,0:T(8,128)S(1)}, s32[]{:T(128)}, s32[]{:T(128)}) while((s32[]{:T(128)}, f32[128,128]{1,0:T(8,128)S(1)}, f32[128,128]{1,0:T(8,128)S(1)}, s32[]{:T(128)}, s32[]{:T(128)}) %tuple.291), condition=%wide.region_22.23_spmd.clone.clone, body=%wide.region_20.22_spmd.clone.clone.sunk | while | flops 34305 | bytes 142421 | solution.py:36
  1676.3 187.1 %while.143 = (s32[]{:T(128)}, f32[128,128]{1,0:T(8,128)S(1)}, f32[128,128]{1,0:T(8,128)S(1)}, s32[]{:T(128)}, s32[]{:T(128)}, /*index=5*/s32[]{:T(128)}, s32[]{:T(128)}) while((s32[]{:T(128)}, f32[128,128]{1,0:T(8,128)S(1)}, f32[128,128]{1,0:T(8,128)S(1)}, s32[]{:T(128)}, s32[]{:T(128)}, /*index=5*/s32[]{:T(128)}, ...), condition=%wide.region_25.26_spmd.clone.clone, body=%wide.region_23.25_spmd.clone.clone.sunk | while | flops 197765 | bytes 69783 | solution.py:52
  1865.1 1.4 fusion.73
  1866.7 1.4 convolution_negate_fusion
  1868.2 8.0 fusion.56
  1876.2 1.1 select_maximum_fusion
  1877.3 0.8 copy-done.1
  1878.1 1.3 copy.83
  (4633 shorter events, 1113.5 us)
Async XLA Ops:
  7.2 164.0 %all-reduce.7.cloned.1.call-start = ((), (), s32[]{:S(2)}) async-start(), calls=%async_computation | async-start | bytes 4194304 | tf_op jit(solution)/shard_map/psum | solution.py:89
  17.4 1.6 copy-start
  17.4 320.2 %all-reduce.9.cloned.1.call-start = ((), (), s32[]{:S(2)}) async-start(), calls=%async_computation.1 | async-start | bytes 2097152 | tf_op jit(solution)/shard_map/psum | solution.py:92
  718.3 0.6 copy-start.2
  1101.5 0.6 copy-start.4
  1482.5 0.6 copy-start.6
  1863.3 1.3 copy-start.8
  1868.1 8.1 copy-start.3
  1868.1 8.1 copy-start.5
  1868.2 8.1 copy-start.7
  1868.2 8.1 copy-start.9
  1876.2 2.0 copy-start.1
Sparse Core Ops, SparseCore 0:
  17.6 153.5 all-reduce.6
  192.0 145.6 all-reduce.8
where the time goes:
time: 1900 us; the launch traced here: 1890 us
  other arithmetic  685 us (36%)
  matrix products  455 us (24%)
  loops' own time  391 us (21%)
  waiting for transfers between devices  296 us (16%)
  local copies, waits for them, and re-layouts  43.5 us (2%)
    dot_general x523, matrix products, product(): jnp.dot(left, right, precision=lax.Precision.HIGHEST, preferred_element_t...  438 us
    another operation x4, loops' own time, small_upper(): return lax.fori_loop(0, width, one_step, start)[1]  377 us
    reduce_sum x512, other arithmetic, one_step(): pivot = jnp.sum(jnp.where(positions == index, row, jnp.float32(0.0)))  311 us
    reduce_sum x512, other arithmetic, one_step(): jnp.sum(jnp.where(positions == column, row, jnp.float32(0.0)))  310 us
    psum x1, waiting for transfers between devices, shards(): coeffs = lax.psum(inner(basis, block), ('leaf', 'side'))  150 us
    psum x1, waiting for transfers between devices, shards(): factor, inverse = factor_and_inverse(lax.psum(local_gram, ('leaf', 'side')))  146 us
    sub x512, other arithmetic, one_step(): rest = rest - new_row[:, None] * new_row[None, :]  42.1 us

commit v1 on v0

v1 whole, which is shorter than its diff:
```python
import functools
import jax
import jax.numpy as jnp
from jax import lax
from jax.experimental import pallas as pl
from jax.experimental.pallas import tpu as pltpu
from jax.sharding import PartitionSpec as P

F32 = jnp.float32
BF16 = jnp.bfloat16
MESH = pl.DeviceIdType.MESH
HI = lax.Precision.HIGHEST
AXES = ((0, 1, 2), (1, 2, 0), (2, 0, 1))


def position():
    leaf, side = lax.axis_index("leaf"), lax.axis_index("side")
    return [leaf // 4, lax.rem(leaf, 4), side // 2], lax.rem(side, 2)


def device(q, core):
    return (q[0] * 4 + q[1], q[2] * 2 + core)


def peer(q, core, axis, k):
    to = list(q)
    to[axis] = lax.rem(q[axis] + k, 4)
    return device(to, core)


def split(v):
    hi = v.astype(BF16)
    return hi, (v - hi.astype(F32)).astype(BF16)


def dot(a, b, dims):
    return lax.dot_general(a, b, (dims, ((), ())), preferred_element_type=F32)


NN, TN, NT = ((1,), (0,)), ((0,), (0,)), ((1,), (1,))


def dot3(ah, al, bh, bl, dims):
    return dot(ah, bh, dims) + (dot(ah, bl, dims) + dot(al, bh, dims))


class Sum:
    def __init__(self, half, streams, x, out, halves, a, y, b, c, sems):
        self.half, self.streams, self.x, self.out = half, streams, x, out
        self.halves, self.a, self.y, self.b, self.c = halves, a, y, b, c
        self.send, self.recv = sems
        self.q, self.core = position()
        self.mine = self.core * half
        self.pending = []

    def copy(self, src, dst, slot, to):
        return pltpu.make_async_remote_copy(
            src_ref=src, dst_ref=dst, send_sem=self.send.at[slot], recv_sem=self.recv.at[slot],
            device_id=to, device_id_type=MESH)

    def start(self, src, dst, slot, to):
        copy = self.copy(src, dst, slot, to)
        copy.start()
        self.pending.append(copy)

    def arrive(self, ref, slot):
        self.copy(ref, ref, slot, device(self.q, 1 - self.core)).wait_recv()

    def rows(self, at, n):
        return pl.ds(pl.multiple_of(at, 8), n)

    def give(self, chunk, off, n):
        src = self.x.at[self.rows((1 - self.core) * self.half + off, n)]
        self.start(src, self.halves.at[pl.ds(off, n)], chunk, device(self.q, 1 - self.core))

    def take(self, chunk, off, n):
        self.arrive(self.halves.at[pl.ds(off, n)], chunk)
        at = self.rows(self.mine + off, n)
        self.x[at, :] += self.halves[pl.ds(off, n), :]

    def slot(self, phase, s, k):
        return 4 + phase * 9 + s * 3 + k - 1

    def phase_a(self, s):
        off, n = self.streams[s]
        axis = AXES[s][0]
        for k in (2, 1, 3):
            part = lax.rem(self.q[axis] + k, 4)
            src = self.x.at[self.rows(self.mine + off + part * (n // 4), n // 4)]
            dst = self.a.at[k - 1, pl.ds(off // 4, n // 4)]
            self.start(src, dst, self.slot(0, s, k), peer(self.q, self.core, axis, k))

    def phase_b(self, s):
        off, n = self.streams[s]
        axis, nxt = AXES[s][0], AXES[s][1]
        at = pl.ds(off // 4, n // 4)
        for k in (1, 3, 2):
            self.arrive(self.a.at[k - 1, at], self.slot(0, s, k))
        own = self.x[self.rows(self.mine + off + self.q[axis] * (n // 4), n // 4), :]
        self.y[at, :] = (own + self.a[0, at, :]) + (self.a[1, at, :] + self.a[2, at, :])
        for k in (2, 1, 3):
            part = lax.rem(self.q[nxt] + k, 4)
            src = self.y.at[at, pl.ds(pl.multiple_of(part * 128, 128), 128)]
            self.start(src, self.b.at[k - 1, at], self.slot(1, s, k), peer(self.q, self.core, nxt, k))

    def phase_c(self, s):
        off, n = self.streams[s]
        axis, nxt = AXES[s][1], AXES[s][2]
        at = pl.ds(off // 4, n // 4)
        for k in (1, 3, 2):
            self.arrive(self.b.at[k - 1, at], self.slot(1, s, k))
        own = self.y[at, pl.ds(pl.multiple_of(self.q[axis] * 128, 128), 128)]
        me = self.q[nxt]
        self.c[me, at, :] = (own + self.b[0, at, :]) + (self.b[1, at, :] + self.b[2, at, :])
        for k in (2, 1, 3):
            self.start(self.c.at[me, at], self.c.at[me, at], self.slot(2, s, k), peer(self.q, self.core, nxt, k))

    def quarter(self, s, part):
        off, n = self.streams[s]
        return self.rows(self.mine + off + part * (n // 4), n // 4)

    def phase_d(self, s):
        off, n = self.streams[s]
        second, third = AXES[s][1], AXES[s][2]
        at = pl.ds(off // 4, n // 4)
        for k in (1, 3, 2):
            self.arrive(self.c.at[lax.rem(self.q[third] + 4 - k, 4), at], self.slot(2, s, k))
        rows = self.quarter(s, self.q[AXES[s][0]])
        columns = pl.ds(pl.multiple_of(self.q[second] * 128, 128), 128)
        self.out[rows, columns] = (self.c[0, at, :] + self.c[1, at, :]) + (self.c[2, at, :] + self.c[3, at, :])
        for k in (2, 1, 3):
            block = self.out.at[rows, columns]
            self.start(block, block, self.slot(3, s, k), peer(self.q, self.core, second, k))

    def phase_e(self, s):
        first, second = AXES[s][0], AXES[s][1]
        rows = self.quarter(s, self.q[first])
        for k in (1, 3, 2):
            part = lax.rem(self.q[second] + 4 - k, 4)
            columns = pl.ds(pl.multiple_of(part * 128, 128), 128)
            self.arrive(self.out.at[rows, columns], self.slot(3, s, k))
        for k in (2, 1, 3):
            self.start(self.out.at[rows], self.out.at[rows], self.slot(4, s, k), peer(self.q, self.core, first, k))
        self.start(self.out.at[rows], self.out.at[rows], 49 + s * 4, device(self.q, 1 - self.core))

    def phase_f(self, s, ks):
        first = AXES[s][0]
        for k in ks:
            rows = self.quarter(s, lax.rem(self.q[first] + 4 - k, 4))
            self.arrive(self.out.at[rows], self.slot(4, s, k))
            self.start(self.out.at[rows], self.out.at[rows], 49 + s * 4 + k, device(self.q, 1 - self.core))

    def finish(self):
        for s, (off, n) in enumerate(self.streams):
            for k in range(4):
                part = lax.rem(self.q[AXES[s][0]] + 4 - k, 4)
                rows = self.rows((1 - self.core) * self.half + off + part * (n // 4), n // 4)
                self.arrive(self.out.at[rows], 49 + s * 4 + k)
        for copy in self.pending:
            copy.wait_send()

    def torus(self):
        for phase in (self.phase_b, self.phase_c, self.phase_d, self.phase_e):
            for s in range(3):
                phase(s)
        for ks in ((1, 3), (2,)):
            for s in range(3):
                self.phase_f(s, ks)
        self.finish()


SEMS = 61
WIDE = ((0, 192), (192, 160), (352, 160))
SMALL = ((0, 64), (64, 64), (128, 64))


def project_kernel(scale, block, basis, ph, pl_, gram, coeffs, sh, sl, kh, kl, x1, h1, a1, y1, b1, c1,
                   x2, h2, a2, y2, b2, c2, send1, recv1, send2, recv2):
    q, core = position()
    barrier = pltpu.get_barrier_semaphore()
    partners = [device(q, 1 - core)] + [peer(q, core, axis, k) for axis in range(3) for k in (1, 2, 3)]
    for to in partners:
        pl.semaphore_signal(barrier, inc=1, device_id=to, device_id_type=MESH)

    @pl.loop(0, 8)
    def _(i):
        at = pl.ds(pl.multiple_of(i * 128, 128), 128)
        hi, lo = split(basis[at, :])
        sh[at, :] = hi
        sl[at, :] = lo
        hi, lo = split(block[at, :])
        kh[at, :] = hi
        kl[at, :] = lo

    def terms(at):
        columns = pl.ds(pl.multiple_of(at, 256), 256)
        x1[columns, :] = dot3(sh[:, columns], sl[:, columns], kh[...], kl[...], TN)

    first = Sum(512, WIDE, x1, coeffs, h1, a1, y1, b1, c1, (send1, recv1))
    for chunk in range(2):
        terms((1 - core) * 512 + chunk * 256)
        if chunk == 0:
            pl.semaphore_wait(barrier, len(partners))
        first.give(chunk, chunk * 256, 256)
    for chunk in range(2):
        terms(core * 512 + chunk * 256)
    first.take(0, 0, 256)
    first.phase_a(0)
    first.take(1, 256, 256)
    first.phase_a(1)
    first.phase_a(2)
    first.torus()

    @pl.loop(0, 4)
    def _(i):
        at = pl.ds(pl.multiple_of(i * 256, 256), 256)
        hi, lo = split(coeffs[at, :])
        kh[at, :] = hi
        kl[at, :] = lo

    @pl.loop(0, 4)
    def _(i):
        at = pl.ds(pl.multiple_of(i * 256, 256), 256)
        hi, lo = split(block[at, :] - dot3(sh[at, :], sl[at, :], kh[...], kl[...], NN))
        ph[at, :] = hi
        pl_[at, :] = lo

    left = pl.ds(0, 256)
    right = pl.ds(256, 256)
    x2[0:256, :] = dot3(ph[:, left], pl_[:, left], ph[...], pl_[...], TN) * scale
    corner = dot3(ph[:, right], pl_[:, right], ph[:, right], pl_[:, right], TN) * scale
    x2[256:384, 0:256] = corner[0:128]
    x2[256:384, 256:512] = corner[128:256]
    second = Sum(192, SMALL, x2, gram, h2, a2, y2, b2, c2, (send2, recv2))
    second.give(0, 0, 192)
    second.take(0, 0, 192)
    for s in range(3):
        second.phase_a(s)
    second.torus()


def buffers(half):
    return [
        pltpu.VMEM((2 * half, 512), F32), pltpu.VMEM((half, 512), F32), pltpu.VMEM((3, half // 4, 512), F32),
        pltpu.VMEM((half // 4, 512), F32), pltpu.VMEM((3, half // 4, 128), F32), pltpu.VMEM((4, half // 4, 128), F32),
    ]


def project(block, basis, rows_total):
    vmem = pl.BlockSpec(memory_space=pltpu.VMEM)
    return pl.pallas_call(
        functools.partial(project_kernel, 1.0 / rows_total),
        out_shape=[
            jax.ShapeDtypeStruct((1024, 512), BF16), jax.ShapeDtypeStruct((1024, 512), BF16),
            jax.ShapeDtypeStruct((384, 512), F32), jax.ShapeDtypeStruct((1024, 512), F32),
        ],
        in_specs=[vmem] * 2,
        out_specs=[vmem] * 4,
        scratch_shapes=[pltpu.VMEM((1024, 1024), BF16)] * 2 + [pltpu.VMEM((1024, 512), BF16)] * 2
        + buffers(512) + buffers(192) + [pltpu.SemaphoreType.DMA((SEMS,))] * 4,
        compiler_params=pltpu.CompilerParams(
            collective_id=0, has_side_effects=True, vmem_limit_bytes=56 * 2**20),
    )(block, basis)


def eliminate(t):
    sub = lax.broadcasted_iota(jnp.int32, (8, 128), 0)
    lane = lax.broadcasted_iota(jnp.int32, (8, 128), 1)
    def row(v, j):
        return jnp.broadcast_to(v[j:j+1, :], (8, 128))
    def col(v, c):
        return jnp.broadcast_to(v[:, c:c+1], (8, 128))
    for p in range(16):
        lo = 8*p
        v0 = t[lo:lo+8, 0:128]
        v1 = t[lo:lo+8, 128:256]
        cs = [col(v0, lo+k) for k in range(8)]
        u0 = v0; u1 = v1
        dm = jnp.ones((8,128), F32); rm = dm
        for j in range(8):
            d = row(cs[j], j)
            r = 1.0/d
            m = jnp.where(sub == j, 0.0, cs[j]*r)
            w0 = row(v0, j); w1 = row(v1, j)
            u0 = jnp.where(sub == j, w0, u0)
            u1 = jnp.where(sub == j, w1, u1)
            dm = jnp.where(sub == j, d, dm)
            rm = jnp.where(sub == j, r, rm)
            for k in range(j+1, 8):
                cs[k] = cs[k] - m*row(cs[k], j)
            v0 = v0 - m*w0
            v1 = v1 - m*w1
        s = jnp.sqrt(dm)
        q = 1.0/s
        t[lo:lo+8, 0:128] = jnp.where(lane >= sub+lo, u0*q, 0.0)
        t[lo:lo+8, 128:256] = u1*q
        z0 = v0*rm; z1 = v1*rm
        zr = [(row(z0,k), row(z1,k)) for k in range(8)]
        for i in range(p+1, 16):
            a0 = t[8*i:8*i+8, 0:128]
            a1 = t[8*i:8*i+8, 128:256]
            ci = [col(a0, lo+k) for k in range(8)]
            s0=[ci[k]*zr[k][0] for k in range(8)]
            s1=[ci[k]*zr[k][1] for k in range(8)]
            while len(s0)>1:
                s0=[s0[2*x]+s0[2*x+1] for x in range(len(s0)//2)]
                s1=[s1[2*x]+s1[2*x+1] for x in range(len(s1)//2)]
            t[8*i:8*i+8, 0:128] = a0 - s0[0]
            t[8*i:8*i+8, 128:256] = a1 - s1[0]


def exact(a, b, dims):
    return lax.dot_general(a, b, (dims, ((), ())), precision=HI, preferred_element_type=F32)


def factor_kernel(g, ph, pl_, coeffs, ortho, r, coeffs_out, s, t, w, sem):
    keep = pltpu.make_async_copy(coeffs, coeffs_out, sem)
    keep.start()
    n = 512
    s[0:256, 0:n] = g[0:256, :]
    s[256:384, 256:n] = g[256:384, 0:256]
    s[384:512, 256:n] = g[256:384, 256:n]
    s[:, n:2 * n] = jnp.zeros((n, n), F32)
    eye = lax.broadcasted_iota(jnp.int32, (128, 128), 0) == lax.broadcasted_iota(jnp.int32, (128, 128), 1)
    eye = jnp.where(eye, 1.0, 0.0)
    for b in range(4):
        s[b * 128 : b * 128 + 128, n + b * 128 : n + b * 128 + 128] = eye
    r[...] = jnp.zeros((n, n), F32)
    w[...] = jnp.zeros((n, n), F32)

    def body(step, carry):
        for b in range(4):
            @pl.when(step == b)
            def _():
                t[:, 0:128] = s[b * 128 : b * 128 + 128, b * 128 : b * 128 + 128]
        t[:, 128:256] = eye
        eliminate(t)
        for b in range(4):
            @pl.when(step == b)
            def _():
                lo, hi = b * 128, b * 128 + 128
                li = t[:, 128:256]
                r[lo:hi, lo:hi] = t[:, 0:128]
                w[lo:hi, lo:hi] = li
                if b:
                    w[lo:hi, 0:lo] = exact(li, s[lo:hi, n : n + lo], NN)
                if b < 3:
                    right = exact(li, s[lo:hi, hi:n], NN)
                    r[lo:hi, hi:n] = right
                    for c in range(b + 1, 4):
                        at = slice(c * 128, c * 128 + 128)
                        rc = right[:, (c - b - 1) * 128 : (c - b) * 128]
                        s[at, c * 128 : n] -= exact(rc, right[:, (c - b - 1) * 128 :], TN)
                        s[at, n : n + hi] -= exact(rc, w[lo:hi, 0:hi], TN)
        return carry

    lax.fori_loop(0, 4, body, 0)
    for c in range(2):
        wh, wl = split(w[c * 256 : c * 256 + 256, 0 : c * 256 + 256])
        k = slice(0, c * 256 + 256)
        ortho[:, c * 256 : c * 256 + 256] = dot3(ph[:, k], pl_[:, k], wh, wl, NT)
    keep.wait()


def orthogonalize(gram, ph, pl_, coeffs):
    vmem = pl.BlockSpec(memory_space=pltpu.VMEM)
    anywhere = pl.BlockSpec(memory_space=pl.ANY)
    return pl.pallas_call(
        factor_kernel,
        out_shape=[
            jax.ShapeDtypeStruct((1024, 512), F32), jax.ShapeDtypeStruct((512, 512), F32),
            jax.ShapeDtypeStruct((1024, 512), F32),
        ],
        in_specs=[vmem] * 3 + [anywhere],
        out_specs=[vmem] * 2 + [anywhere],
        scratch_shapes=[
            pltpu.VMEM((512, 1024), F32), pltpu.VMEM((128, 256), F32), pltpu.VMEM((512, 512), F32),
            pltpu.SemaphoreType.DMA,
        ],
        compiler_params=pltpu.CompilerParams(vmem_limit_bytes=48 * 2**20),
    )(gram, ph, pl_, coeffs)


def shards(block, basis):
    rows_total = block.shape[0] * lax.axis_size("leaf") * lax.axis_size("side")
    ph, pl_, gram, coeffs = project(block, basis, rows_total)
    return orthogonalize(gram, ph, pl_, coeffs)


def solution(mesh):
    return jax.shard_map(
        shards,
        mesh=mesh,
        in_specs=(P(("leaf", "side"), None), P(("leaf", "side"), None)),
        out_specs=(P(("leaf", "side"), None), P(), P()),
        check_vma=False,
    )
```

time: 1900 us -> 101 us (0.05)
  other arithmetic: 685 us -> 0 us
  matrix products: 455 us -> 0 us
  loops' own time: 391 us -> 0 us
  waiting for transfers between devices: 296 us -> 0 us
  Pallas kernels: 0 us -> 95.1 us
  local copies, waits for them, and re-layouts: 43.5 us -> 5.17 us
    reduce_sum x1024 -> x0, other arithmetic: 621 us -> none  [the longest x512 311 us: one_step(): pivot = jnp.sum(jnp.where(positions == index, row, jnp.float32(0.0)))]
    dot_general x528 -> x0, matrix products: 455 us -> none  [the longest x523 438 us: product(): jnp.dot(left, right, precision=lax.Precision.HIGHEST, preferred_element_t...]
    another operation x8 -> x0, loops' own time: 391 us -> none  [the longest x4 377 us: small_upper(): return lax.fori_loop(0, width, one_step, start)[1]]
    psum x2 -> x0, waiting for transfers between devices: 296 us -> none  [the longest x1 150 us: shards(): coeffs = lax.psum(inner(basis, block), ('leaf', 'side'))]
    pallas_call x0 -> x2, Pallas kernels: none -> 95.1 us  [the longest x1 70.5 us: project(): pl.pallas_call(functools.partial(project_kernel, 1.0 / rows_total), out_s...]
    sub x512 -> x0, other arithmetic: 42.1 us -> none  [one_step(): rest = rest - new_row[:, None] * new_row[None, :]]
    dynamic_update_slice x1024 -> x0, local copies, waits for them, and re-layouts: 35 us -> none  [the longest x512 19.1 us: one_step(): lax.dynamic_update_slice_in_dim(result, new_row[None, :], column, 0)]
where the time goes in v1:
time: 101 us
  Pallas kernels  95.1 us (94%)
  local copies, waits for them, and re-layouts  5.17 us (5%)
    pallas_call x1, Pallas kernels, project(): pl.pallas_call(functools.partial(project_kernel, 1.0 / rows_total), out_s...  70.5 us
    pallas_call x1, Pallas kernels, orthogonalize(): pl.pallas_call(factor_kernel, out_shape=[jax.ShapeDtypeStruct((1024, 512)...  24.6 us
    unnamed x8, local copies, waits for them, and re-layouts  5.17 us

profile of v1, /device:TPU:1, one launch (start us, length us, event | category | flops | bytes accessed | tf_op | source)
XLA Modules:
  0.0 100.9 jit_solution(11863869218623779892)
XLA Ops:
  0.6 70.5 %shard_map.49 = (bf16[1024,512]{1,0:T(8,128)(2,1)}, bf16[1024,512]{1,0:T(8,128)(2,1)}, f32[384,512]{1,0:T(8,128)}, f32[1024,512]{1,0:T(8,128)}) custom-call(f32[1024,512]{1,0:T(8,128)} %block.1, f32[1024,1024]{1,0:T(8,128)} %basis.1), custom_call_target="tpu_custom_call" | custom-call | tf_op jit(solution)/shard_map/pallas_call | solution.py:251
  71.1 0.0 copy-start
  71.1 1.6 %copy-done = f32[1024,512]{1,0:T(8,128)S(1)} copy-done((f32[1024,512]{1,0:T(8,128)S(1)}, f32[1024,512]{1,0:T(8,128)}, u32[]{:S(2)}) %copy-start) | copy-done | bytes 2097176
  72.7 0.0 copy-start.1
  72.7 1.2 %copy-done.1 = bf16[1024,512]{1,0:T(8,128)(2,1)S(1)} copy-done((bf16[1024,512]{1,0:T(8,128)(2,1)S(1)}, bf16[1024,512]{1,0:T(8,128)(2,1)}, u32[]{:S(2)}) %copy-start.1) | copy-done | bytes 1048600
  73.9 0.0 copy-start.2
  73.9 1.2 %copy-done.2 = bf16[1024,512]{1,0:T(8,128)(2,1)S(1)} copy-done((bf16[1024,512]{1,0:T(8,128)(2,1)S(1)}, bf16[1024,512]{1,0:T(8,128)(2,1)}, u32[]{:S(2)}) %copy-start.2) | copy-done | bytes 1048600
  75.2 0.0 copy-start.3
  75.2 1.1 %copy-done.3 = f32[384,512]{1,0:T(8,128)S(1)} copy-done((f32[384,512]{1,0:T(8,128)S(1)}, f32[384,512]{1,0:T(8,128)}, u32[]{:S(2)}) %copy-start.3) | copy-done | bytes 786456
  76.3 24.6 %shard_map.50 = (f32[1024,512]{1,0:T(8,128)}, f32[512,512]{1,0:T(8,128)}, f32[1024,512]{1,0:T(8,128)}) custom-call(f32[384,512]{1,0:T(8,128)S(1)} %copy-done.3, bf16[1024,512]{1,0:T(8,128)(2,1)S(1)} %copy-done.1, bf16[1024,512]{1,0:T(8,128)(2,1)S(1)} %copy-done.2, f32[1024,512]{1,0:T(8,128)S(1)} %copy-done), custom_call_target="tpu_custom_call" | custom-call | tf_op jit(solution)/shard_map/pallas_call | solution.py:368
Async XLA Ops:
  71.1 1.6 %copy-start = (f32[1024,512]{1,0:T(8,128)S(1)}, f32[1024,512]{1,0:T(8,128)}, u32[]{:S(2)}) copy-start(f32[1024,512]{1,0:T(8,128)} %get-tuple-element.10.coeffs) | copy-start | bytes 6291460
  72.7 1.2 %copy-start.1 = (bf16[1024,512]{1,0:T(8,128)(2,1)S(1)}, bf16[1024,512]{1,0:T(8,128)(2,1)}, u32[]{:S(2)}) copy-start(bf16[1024,512]{1,0:T(8,128)(2,1)} %get-tuple-element.8.ph) | copy-start | bytes 3145732
  73.9 1.2 %copy-start.2 = (bf16[1024,512]{1,0:T(8,128)(2,1)S(1)}, bf16[1024,512]{1,0:T(8,128)(2,1)}, u32[]{:S(2)}) copy-start(bf16[1024,512]{1,0:T(8,128)(2,1)} %get-tuple-element.9.pl_) | copy-start | bytes 3145732
  75.2 1.1 %copy-start.3 = (f32[384,512]{1,0:T(8,128)S(1)}, f32[384,512]{1,0:T(8,128)}, u32[]{:S(2)}) copy-start(f32[384,512]{1,0:T(8,128)} %get-tuple-element.7.g) | copy-start | bytes 2359300

commit v2 on v1

v2 whole, which is shorter than its diff:
```python
import functools
import jax
import jax.numpy as jnp
from jax import lax
from jax.experimental import pallas as pl
from jax.experimental.pallas import tpu as pltpu
from jax.sharding import PartitionSpec as P

F32 = jnp.float32
BF16 = jnp.bfloat16
MESH = pl.DeviceIdType.MESH
HI = lax.Precision.HIGHEST
AXES = ((0, 1, 2), (1, 2, 0), (2, 0, 1))


def position():
    leaf, side = lax.axis_index("leaf"), lax.axis_index("side")
    return [leaf // 4, lax.rem(leaf, 4), side // 2], lax.rem(side, 2)


def device(q, core):
    return (q[0] * 4 + q[1], q[2] * 2 + core)


def peer(q, core, axis, k, second=None, k2=0):
    to = list(q)
    to[axis] = lax.rem(q[axis] + k, 4)
    if second is not None:
        to[second] = lax.rem(q[second] + k2, 4)
    return device(to, core)


def split(v):
    hi = v.astype(BF16)
    return hi, (v - hi.astype(F32)).astype(BF16)


def dot(a, b, dims):
    return lax.dot_general(a, b, (dims, ((), ())), preferred_element_type=F32)


NN, TN, NT = ((1,), (0,)), ((0,), (0,)), ((1,), (1,))


def dot3(ah, al, bh, bl, dims):
    return dot(ah, bh, dims) + (dot(ah, bl, dims) + dot(al, bh, dims))


class Sum:
    def __init__(self, half, stride, base, streams, x, out, halves, a, y, b, c, send, recv):
        self.half, self.streams, self.x, self.out = half, streams, x, out
        self.halves, self.a, self.y, self.b, self.c = halves, a, y, b, c
        self.send, self.recv = send, recv
        self.q, self.core = position()
        self.mine = self.core * stride + base
        self.other = (1 - self.core) * stride + base
        self.pending = []

    def copy(self, src, dst, slot, to):
        return pltpu.make_async_remote_copy(
            src_ref=src, dst_ref=dst, send_sem=self.send.at[slot], recv_sem=self.recv.at[slot],
            device_id=to, device_id_type=MESH)

    def start(self, src, dst, slot, to):
        copy = self.copy(src, dst, slot, to)
        copy.start()
        self.pending.append(copy)

    def arrive(self, ref, slot):
        self.copy(ref, ref, slot, device(self.q, 1 - self.core)).wait_recv()

    def rows(self, at, n):
        return pl.ds(pl.multiple_of(at, 8), n)

    def give(self):
        chunk, off, n = 0, 0, self.half
        src = self.x.at[self.rows(self.other + off, n)]
        self.start(src, self.halves.at[pl.ds(off, n)], chunk, device(self.q, 1 - self.core))

    def take(self):
        chunk, off, n = 0, 0, self.half
        self.arrive(self.halves.at[pl.ds(off, n)], chunk)
        at = self.rows(self.mine + off, n)
        self.x[at, :] += self.halves[pl.ds(off, n), :]

    def slot(self, phase, s, k):
        return 4 + phase * 9 + s * 3 + k - 1

    def phase_a(self, s):
        off, n = self.streams[s]
        axis = AXES[s][0]
        for k in (2, 1, 3):
            part = lax.rem(self.q[axis] + k, 4)
            src = self.x.at[self.rows(self.mine + off + part * (n // 4), n // 4)]
            dst = self.a.at[k - 1, pl.ds(off // 4, n // 4)]
            self.start(src, dst, self.slot(0, s, k), peer(self.q, self.core, axis, k))

    def phase_b(self, s):
        off, n = self.streams[s]
        axis, nxt = AXES[s][0], AXES[s][1]
        at = pl.ds(off // 4, n // 4)
        for k in (1, 3, 2):
            self.arrive(self.a.at[k - 1, at], self.slot(0, s, k))
        own = self.x[self.rows(self.mine + off + self.q[axis] * (n // 4), n // 4), :]
        self.y[at, :] = (own + self.a[0, at, :]) + (self.a[1, at, :] + self.a[2, at, :])
        for k in (2, 1, 3):
            part = lax.rem(self.q[nxt] + k, 4)
            src = self.y.at[at, pl.ds(pl.multiple_of(part * 128, 128), 128)]
            self.start(src, self.b.at[k - 1, at], self.slot(1, s, k), peer(self.q, self.core, nxt, k))

    def phase_c(self, s):
        off, n = self.streams[s]
        axis, nxt = AXES[s][1], AXES[s][2]
        at = pl.ds(off // 4, n // 4)
        for k in (1, 3, 2):
            self.arrive(self.b.at[k - 1, at], self.slot(1, s, k))
        own = self.y[at, pl.ds(pl.multiple_of(self.q[axis] * 128, 128), 128)]
        me = self.q[nxt]
        self.c[me, at, :] = (own + self.b[0, at, :]) + (self.b[1, at, :] + self.b[2, at, :])
        for k in (2, 1, 3):
            self.start(self.c.at[me, at], self.c.at[me, at], self.slot(2, s, k), peer(self.q, self.core, nxt, k))

    def quarter(self, s, part):
        off, n = self.streams[s]
        return self.rows(self.mine + off + part * (n // 4), n // 4)

    def phase_d(self, s):
        off, n = self.streams[s]
        second, third = AXES[s][1], AXES[s][2]
        at = pl.ds(off // 4, n // 4)
        for k in (1, 3, 2):
            self.arrive(self.c.at[lax.rem(self.q[third] + 4 - k, 4), at], self.slot(2, s, k))
        rows = self.quarter(s, self.q[AXES[s][0]])
        columns = pl.ds(pl.multiple_of(self.q[second] * 128, 128), 128)
        self.out[rows, columns] = (self.c[0, at, :] + self.c[1, at, :]) + (self.c[2, at, :] + self.c[3, at, :])
        for k in (2, 1, 3):
            block = self.out.at[rows, columns]
            self.start(block, block, self.slot(3, s, k), peer(self.q, self.core, second, k))

    def phase_e(self, s):
        first, second = AXES[s][0], AXES[s][1]
        rows = self.quarter(s, self.q[first])
        for k in (1, 3, 2):
            part = lax.rem(self.q[second] + 4 - k, 4)
            columns = pl.ds(pl.multiple_of(part * 128, 128), 128)
            self.arrive(self.out.at[rows, columns], self.slot(3, s, k))
        for k in (2, 1, 3):
            self.start(self.out.at[rows], self.out.at[rows], self.slot(4, s, k), peer(self.q, self.core, first, k))
        self.start(self.out.at[rows], self.out.at[rows], 49 + s * 4, device(self.q, 1 - self.core))

    def phase_f(self, s, ks):
        first = AXES[s][0]
        for k in ks:
            rows = self.quarter(s, lax.rem(self.q[first] + 4 - k, 4))
            self.arrive(self.out.at[rows], self.slot(4, s, k))
            self.start(self.out.at[rows], self.out.at[rows], 49 + s * 4 + k, device(self.q, 1 - self.core))

    def meet(self):
        for s, (off, n) in enumerate(self.streams):
            for k in range(4):
                part = lax.rem(self.q[AXES[s][0]] + 4 - k, 4)
                self.arrive(self.out.at[self.rows(self.other + off + part * (n // 4), n // 4)], 49 + s * 4 + k)

    def drain(self):
        for copy in self.pending:
            copy.wait_send()


class PlaneSum(Sum):
    def plane(self, gather, s, k, k2):
        return 61 + gather * 45 + s * 15 + k * 4 + k2 - 1

    def scatter(self, s):
        off, n = self.streams[s]
        first, second = AXES[s][0], AXES[s][1]
        at = pl.ds(off // 4, n // 4)
        for k, k2 in STEPS:
            rows = self.quarter(s, lax.rem(self.q[first] + k, 4), self.x)
            columns = self.columns(lax.rem(self.q[second] + k2, 4))
            self.start(self.x.at[rows, columns], self.b.at[k * 4 + k2 - 1, at], self.plane(0, s, k, k2),
                       peer(self.q, self.core, first, k, second, k2))

    def columns(self, part):
        return pl.ds(pl.multiple_of(part * 128, 128), 128)

    def quarter(self, s, part, ref=None):
        off, n = self.streams[s]
        return self.rows(self.mine + off + part * (n // 4), n // 4)

    def exchange(self, s):
        off, n = self.streams[s]
        first, second, third = AXES[s]
        at = pl.ds(off // 4, n // 4)
        for k, k2 in STEPS[::-1]:
            self.arrive(self.b.at[k * 4 + k2 - 1, at], self.plane(0, s, k, k2))
        parts = [self.b[i, at, :] for i in range(15)]
        parts.append(self.x[self.quarter(s, self.q[first]), self.columns(self.q[second])])
        while len(parts) > 1:
            parts = [parts[i] + parts[i + 1] for i in range(0, len(parts), 2)]
        me = self.q[third]
        self.c[me, at, :] = parts[0]
        for k in (2, 1, 3):
            self.start(self.c.at[me, at], self.c.at[me, at], self.slot(2, s, k), peer(self.q, self.core, third, k))

    def gather(self, s):
        off, n = self.streams[s]
        first, second, third = AXES[s]
        at = pl.ds(off // 4, n // 4)
        for k in (1, 3, 2):
            self.arrive(self.c.at[lax.rem(self.q[third] + 4 - k, 4), at], self.slot(2, s, k))
        block = self.out.at[self.quarter(s, self.q[first]), self.columns(self.q[second])]
        block[...] = (self.c[0, at, :] + self.c[1, at, :]) + (self.c[2, at, :] + self.c[3, at, :])
        for k, k2 in STEPS:
            self.start(block, block, self.plane(1, s, k, k2), peer(self.q, self.core, first, k, second, k2))

    def forward(self, s, ks):
        first, second = AXES[s][0], AXES[s][1]
        for k in ks:
            rows = self.quarter(s, lax.rem(self.q[first] + 4 - k, 4))
            for k2 in (0, 1, 3, 2):
                if k or k2:
                    block = self.out.at[rows, self.columns(lax.rem(self.q[second] + 4 - k2, 4))]
                    self.arrive(block, self.plane(1, s, k, k2))
            self.start(self.out.at[rows], self.out.at[rows], 49 + s * 4 + k, device(self.q, 1 - self.core))


STEPS = tuple((k, k2) for k in (2, 1, 3, 0) for k2 in (2, 1, 3, 0) if k or k2)


WIDE = ((0, 96), (96, 96), (192, 64))
SMALL = ((0, 64), (64, 64), (128, 64))


def project_kernel(scale, block_in, basis_in, ph_out, pl_out, gram, coeffs_out, bs, bk, sh, sl, kh, kl, ph, pl_, x1, coeffs, x2,
                   load, *rest):
    buffers0, buffers1, buffers2, store = rest[0:7], rest[7:14], rest[14:20], rest[20]
    q, core = position()
    loads = []
    for i in range(4):
        at = pl.ds(i * 256, 256)
        loads.append((pltpu.make_async_copy(basis_in.at[at], bs.at[at], load.at[0, i]),
                      pltpu.make_async_copy(block_in.at[at], bk.at[at], load.at[1, i])))
    for pair in loads:
        for copy in pair:
            copy.start()
    barrier = pltpu.get_barrier_semaphore()
    partners = [device(q, 1 - core)] + [peer(q, core, axis, k) for axis in range(3) for k in (1, 2, 3)]
    partners += [peer(q, core, first, k, second, k2) for first, second, _ in AXES for k in (1, 2, 3) for k2 in (1, 2, 3)]
    for to in partners:
        pl.semaphore_signal(barrier, inc=1, device_id=to, device_id_type=MESH)

    for i in range(4):
        for copy in loads[i]:
            copy.wait()

        @pl.loop(i * 2, i * 2 + 2)
        def _(j):
            at = pl.ds(pl.multiple_of(j * 128, 128), 128)
            hi, lo = split(bs[at, :])
            sh[at, :] = hi
            sl[at, :] = lo
            hi, lo = split(bk[at, :])
            kh[at, :] = hi
            kl[at, :] = lo

    def terms(at):
        columns = pl.ds(pl.multiple_of(at, 256), 256)
        x1[columns, :] = dot3(sh[:, columns], sl[:, columns], kh[...], kl[...], TN)

    sums = [Sum(256, 512, 256 * i, WIDE, x1, coeffs, *half) for i, half in enumerate((buffers0[:7], buffers1[:7]))]
    for i in range(2):
        terms((1 - core) * 512 + i * 256)
        if i == 0:
            pl.semaphore_wait(barrier, len(partners))
        sums[i].give()
    for i in range(2):
        terms(core * 512 + i * 256)
        sums[i].take()
        for s in range(3):
            sums[i].phase_a(s)
    for phase in ("phase_b", "phase_c", "phase_d", "phase_e"):
        for each in sums:
            for s in range(3):
                getattr(each, phase)(s)

    def subtract(at):
        rows = pl.ds(pl.multiple_of(at, 256), 256)
        hi, lo = split(coeffs[rows, :])
        kh[rows, :] = hi
        kl[rows, :] = lo

        @pl.loop(0, 4)
        def _(i):
            at = pl.ds(pl.multiple_of(i * 256, 256), 256)
            bk[at, :] -= dot3(sh[at, rows], sl[at, rows], kh[rows, :], kl[rows, :], NN)

    for i in range(2):
        for ks in ((1, 3), (2,)):
            for s in range(3):
                sums[i].phase_f(s, ks)
        subtract(core * 512 + i * 256)
    for i in range(2):
        sums[i].meet()
        subtract((1 - core) * 512 + i * 256)

    keep = [pltpu.make_async_copy(coeffs, coeffs_out, store.at[0])]
    keep[0].start()

    @pl.loop(0, 4)
    def _(i):
        at = pl.ds(pl.multiple_of(i * 256, 256), 256)
        hi, lo = split(bk[at, :])
        ph[at, :] = hi
        pl_[at, :] = lo

    keep += [pltpu.make_async_copy(ph, ph_out, store.at[1]), pltpu.make_async_copy(pl_, pl_out, store.at[2])]
    keep[1].start()
    keep[2].start()
    left = pl.ds(0, 256)
    right = pl.ds(256, 256)
    x2[0:256, :] = dot3(ph[:, left], pl_[:, left], ph[...], pl_[...], TN) * scale
    corner = dot3(ph[:, right], pl_[:, right], ph[:, right], pl_[:, right], TN) * scale
    x2[256:384, 0:256] = corner[0:128]
    x2[256:384, 256:512] = corner[128:256]
    halves, b, c, send, recv = buffers2[0], buffers2[1], buffers2[2], buffers2[3], buffers2[4]
    last = PlaneSum(192, 192, 0, SMALL, x2, gram, halves, None, None, b, c, send, recv)
    last.give()
    last.take()
    for phase in (last.scatter, last.exchange, last.gather):
        for s in range(3):
            phase(s)
    for ks in ((0, 1, 3), (2,)):
        for s in range(3):
            last.forward(s, ks)
    last.meet()
    for each in (*sums, last):
        each.drain()
    for copy in keep:
        copy.wait()


def buffers(half):
    return [
        pltpu.VMEM((half, 512), F32), pltpu.VMEM((3, half // 4, 512), F32), pltpu.VMEM((half // 4, 512), F32),
        pltpu.VMEM((3, half // 4, 128), F32), pltpu.VMEM((4, half // 4, 128), F32),
        pltpu.SemaphoreType.DMA((61,)), pltpu.SemaphoreType.DMA((61,)),
    ]


def project(block, basis, rows_total):
    anywhere = pl.BlockSpec(memory_space=pl.ANY)
    return pl.pallas_call(
        functools.partial(project_kernel, 1.0 / rows_total),
        out_shape=[
            jax.ShapeDtypeStruct((1024, 512), BF16), jax.ShapeDtypeStruct((1024, 512), BF16),
            jax.ShapeDtypeStruct((384, 512), F32), jax.ShapeDtypeStruct((1024, 512), F32),
        ],
        in_specs=[anywhere] * 2,
        out_specs=[anywhere, anywhere, pl.BlockSpec(memory_space=pltpu.VMEM), anywhere],
        scratch_shapes=[
            pltpu.VMEM((1024, 1024), F32), pltpu.VMEM((1024, 512), F32),
            pltpu.VMEM((1024, 1024), BF16), pltpu.VMEM((1024, 1024), BF16),
            pltpu.VMEM((1024, 512), BF16), pltpu.VMEM((1024, 512), BF16),
            pltpu.VMEM((1024, 512), BF16), pltpu.VMEM((1024, 512), BF16),
            pltpu.VMEM((1024, 512), F32), pltpu.VMEM((1024, 512), F32), pltpu.VMEM((384, 512), F32),
            pltpu.SemaphoreType.DMA((2, 4)),
            *buffers(256), *buffers(256),
            pltpu.VMEM((192, 512), F32), pltpu.VMEM((15, 48, 128), F32), pltpu.VMEM((4, 48, 128), F32),
            pltpu.SemaphoreType.DMA((151,)), pltpu.SemaphoreType.DMA((151,)), pltpu.SemaphoreType.DMA((1,)),
            pltpu.SemaphoreType.DMA((3,)),
        ],
        compiler_params=pltpu.CompilerParams(
            collective_id=0, has_side_effects=True, vmem_limit_bytes=60 * 2**20),
    )(block, basis)


def eliminate(t):
    sub = lax.broadcasted_iota(jnp.int32, (8, 128), 0)
    lane = lax.broadcasted_iota(jnp.int32, (8, 128), 1)

    def row(v, j):
        return jnp.broadcast_to(v[j : j + 1, :], (8, 128))

    def col(v, c):
        return jnp.broadcast_to(v[:, c : c + 1], (8, 128))

    def update(i, lo, zr):
        a0 = t[8 * i : 8 * i + 8, 0:128]
        a1 = t[8 * i : 8 * i + 8, 128:256]
        ci = [col(a0, lo + k) for k in range(8)]
        s0 = [ci[k] * zr[k][0] for k in range(8)]
        s1 = [ci[k] * zr[k][1] for k in range(8)]
        while len(s0) > 1:
            s0 = [s0[x] + s0[x + 1] for x in range(0, len(s0), 2)]
            s1 = [s1[x] + s1[x + 1] for x in range(0, len(s1), 2)]
        v0, v1 = a0 - s0[0], a1 - s1[0]
        t[8 * i : 8 * i + 8, 0:128] = v0
        t[8 * i : 8 * i + 8, 128:256] = v1
        return v0, v1

    v0, v1 = t[0:8, 0:128], t[0:8, 128:256]
    for p in range(16):
        lo = 8 * p
        x = [col(v0, lo + k) for k in range(8)] + [v0, v1]
        raw0, raw1 = v0, v1
        a_of = jnp.ones((8, 128), F32)
        b_of = jnp.zeros((8, 128), F32)
        d_of = b_of
        for j in range(0, 8, 2):
            even, odd = sub == j, sub == j + 1
            pair = even | odd
            top = [row(v, j) if n > j else None for n, v in enumerate(x)]
            low = [row(v, j + 1) if n > j else None for n, v in enumerate(x)]
            a, b, c = row(x[j], j), top[j + 1], low[j + 1]
            g = 1.0 / (a * c - b * b)
            n0 = jnp.where(even, c, jnp.where(odd, -b, x[j + 1] * b - x[j] * c))
            n1 = jnp.where(even, -b, jnp.where(odd, a, x[j] * b - x[j + 1] * a))
            raw0 = jnp.where(even, top[8], jnp.where(odd, low[8], raw0))
            raw1 = jnp.where(even, top[9], jnp.where(odd, low[9], raw1))
            a_of = jnp.where(odd, a, a_of)
            b_of = jnp.where(odd, b, b_of)
            d_of = jnp.where(even, a, jnp.where(odd, c, d_of))
            for n in range(j + 2, 10):
                x[n] = jnp.where(pair, 0.0, x[n]) + g * (n0 * top[n] + n1 * low[n])
        zr = [(row(x[8], k), row(x[9], k)) for k in range(8)]
        if p < 15:
            v0, v1 = update(p + 1, lo, zr)
        m = b_of / a_of
        q = 1.0 / jnp.sqrt(d_of - m * b_of)
        u0 = raw0 - m * pltpu.roll(raw0, 1, 0)
        u1 = raw1 - m * pltpu.roll(raw1, 1, 0)
        t[lo : lo + 8, 0:128] = jnp.where(lane >= sub + lo, u0 * q, 0.0)
        t[lo : lo + 8, 128:256] = u1 * q
        for i in range(p + 2, 16):
            update(i, lo, zr)


def exact(a, b, dims):
    return lax.dot_general(a, b, (dims, ((), ())), precision=HI, preferred_element_type=F32)


def factor_kernel(g_in, ph_in, pl_in, coeffs, ortho_out, r_out, coeffs_out, g, ph, pl_, ortho, r, s, t, w, root, sems):
    copies = [pltpu.make_async_copy(a, b, sems.at[i]) for i, (a, b) in enumerate(
        ((g_in, g), (ph_in, ph), (pl_in, pl_), (coeffs, coeffs_out)))]
    for copy in copies:
        copy.start()
    n = 512
    r[...] = jnp.zeros((n, n), F32)
    w[...] = jnp.zeros((n, n), F32)
    s[:, n : 2 * n] = jnp.zeros((n, n), F32)
    eye = lax.broadcasted_iota(jnp.int32, (128, 128), 0) == lax.broadcasted_iota(jnp.int32, (128, 128), 1)
    copies[0].wait()
    s[0:256, 0:n] = g[0:256, :]
    s[256:384, 256:n] = g[256:384, 0:256]
    s[384:512, 256:n] = g[256:384, 256:n]
    down = []
    for b in range(4):
        at = slice(b * 128, b * 128 + 128)
        diagonal = jnp.where(eye, s[at, at], 0.0)
        across = jnp.sqrt(jnp.sum(diagonal, axis=0, keepdims=True))
        root[0:1, at] = across
        root[1:2, at] = 1.0 / across
        s[at, n + b * 128 : n + b * 128 + 128] = jnp.where(eye, 1.0 / across, 0.0)
        down.append(1.0 / jnp.sqrt(jnp.sum(diagonal, axis=1, keepdims=True)))
    for b in range(4):
        at = slice(b * 128, b * 128 + 128)
        s[at, b * 128 : n] = s[at, b * 128 : n] * down[b] * root[1:2, b * 128 : n]

    def body(step, carry):
        for b in range(4):
            @pl.when(step == b)
            def _():
                t[:, 0:128] = s[b * 128 : b * 128 + 128, b * 128 : b * 128 + 128]
                t[:, 128:256] = s[b * 128 : b * 128 + 128, n + b * 128 : n + b * 128 + 128]
        eliminate(t)
        for b in range(4):
            @pl.when(step == b)
            def _():
                lo, hi = b * 128, b * 128 + 128
                scaled = t[:, 128:256]
                li = scaled * root[0:1, lo:hi]
                r[lo:hi, lo:hi] = t[:, 0:128] * root[0:1, lo:hi]
                w[lo:hi, lo:hi] = scaled
                if b:
                    w[lo:hi, 0:lo] = exact(li, s[lo:hi, n : n + lo], NN)
                if b < 3:
                    right = exact(li, s[lo:hi, hi:n], NN)
                    r[lo:hi, hi:n] = right * root[0:1, hi:n]
                    for c in range(b + 1, 4):
                        at = slice(c * 128, c * 128 + 128)
                        rc = right[:, (c - b - 1) * 128 : (c - b) * 128]
                        s[at, c * 128 : n] -= exact(rc, right[:, (c - b - 1) * 128 :], TN)
                        s[at, n : n + hi] -= exact(rc, w[lo:hi, 0:hi], TN)
        return carry

    lax.fori_loop(0, 4, body, 0)
    stores = [pltpu.make_async_copy(r, r_out, sems.at[4])]
    stores[0].start()
    copies[1].wait()
    copies[2].wait()
    wh, wl = split(w[...])
    for i in range(4):
        rows = slice(i * 256, i * 256 + 256)
        for c in range(2):
            at, k = slice(c * 256, c * 256 + 256), slice(0, c * 256 + 256)
            ortho[rows, at] = dot3(ph[rows, k], pl_[rows, k], wh[at, k], wl[at, k], NT)
        stores.append(pltpu.make_async_copy(ortho.at[pl.ds(i * 256, 256)], ortho_out.at[pl.ds(i * 256, 256)], sems.at[5 + i]))
        stores[-1].start()
    copies[3].wait()
    for copy in stores:
        copy.wait()


def orthogonalize(gram, ph, pl_, coeffs):
    anywhere = pl.BlockSpec(memory_space=pl.ANY)
    return pl.pallas_call(
        factor_kernel,
        out_shape=[
            jax.ShapeDtypeStruct((1024, 512), F32), jax.ShapeDtypeStruct((512, 512), F32),
            jax.ShapeDtypeStruct((1024, 512), F32),
        ],
        in_specs=[anywhere] * 4,
        out_specs=[anywhere] * 3,
        scratch_shapes=[
            pltpu.VMEM((384, 512), F32), pltpu.VMEM((1024, 512), BF16), pltpu.VMEM((1024, 512), BF16),
            pltpu.VMEM((1024, 512), F32), pltpu.VMEM((512, 512), F32),
            pltpu.VMEM((512, 1024), F32), pltpu.VMEM((128, 256), F32), pltpu.VMEM((512, 512), F32),
            pltpu.VMEM((8, 512), F32), pltpu.SemaphoreType.DMA((9,)),
        ],
        compiler_params=pltpu.CompilerParams(vmem_limit_bytes=63 * 2**20),
    )(gram, ph, pl_, coeffs)


def shards(block, basis):
    rows_total = block.shape[0] * lax.axis_size("leaf") * lax.axis_size("side")
    ph, pl_, gram, coeffs = project(block, basis, rows_total)
    return orthogonalize(gram, ph, pl_, coeffs)


def solution(mesh):
    return jax.shard_map(
        shards,
        mesh=mesh,
        in_specs=(P(("leaf", "side"), None), P(("leaf", "side"), None)),
        out_specs=(P(("leaf", "side"), None), P(), P()),
        check_vma=False,
    )
```

time: 101 us -> 129 us (1.28)
  Pallas kernels: 95.1 us -> 128 us
  local copies, waits for them, and re-layouts: 5.17 us -> 0 us
    pallas_call x1, Pallas kernels: 24.6 us -> 64.7 us  [orthogonalize(): pl.pallas_call(factor_kernel, out_shape=[jax.ShapeDtypeStruct((1024, 512)...]
    pallas_call x1, Pallas kernels: 70.5 us -> 63.3 us  [project(): pl.pallas_call(functools.partial(project_kernel, 1.0 / rows_total), out_s...]
    unnamed x8 -> x0, local copies, waits for them, and re-layouts: 5.17 us -> none
where the time goes in v2:
time: 129 us
  Pallas kernels  128 us (99%)
    pallas_call x1, Pallas kernels, orthogonalize(): pl.pallas_call(factor_kernel, out_shape=[jax.ShapeDtypeStruct((1024, 512)...  64.7 us
    pallas_call x1, Pallas kernels, project(): pl.pallas_call(functools.partial(project_kernel, 1.0 / rows_total), out_s...  63.3 us

profile of v2, /device:TPU:1, one launch (start us, length us, event | category | flops | bytes accessed | tf_op | source)
XLA Modules:
  0.0 128.9 jit_solution(5750792524082109974)
XLA Ops:
  0.6 63.3 %shard_map.49 = (bf16[1024,512]{1,0:T(8,128)(2,1)}, bf16[1024,512]{1,0:T(8,128)(2,1)}, f32[384,512]{1,0:T(8,128)}, f32[1024,512]{1,0:T(8,128)}) custom-call(f32[1024,512]{1,0:T(8,128)} %block_in.1, f32[1024,1024]{1,0:T(8,128)} %basis_in.1), custom_call_target="tpu_custom_call" | custom-call | tf_op jit(solution)/shard_map/pallas_call | solution.py:352
  64.0 64.7 %shard_map.50 = (f32[1024,512]{1,0:T(8,128)}, f32[512,512]{1,0:T(8,128)}, f32[1024,512]{1,0:T(8,128)}) custom-call(f32[384,512]{1,0:T(8,128)} %get-tuple-element.7.g_in, bf16[1024,512]{1,0:T(8,128)(2,1)} %get-tuple-element.8.ph_in, bf16[1024,512]{1,0:T(8,128)(2,1)} %get-tuple-element.9.pl_in, f32[1024,512]{1,0:T(8,128)} %get-tuple-element.10.coeffs), custom_call_target="tpu_custom_call" | custom-call | tf_op jit(solution)/shard_map/pallas_call | solution.py:516

commit v3 on v2

--- a/solution.py
+++ b/solution.py
@@ -439,9 +439,9 @@
     return lax.dot_general(a, b, (dims, ((), ())), precision=HI, preferred_element_type=F32)
 
 
-def factor_kernel(g_in, ph_in, pl_in, coeffs, ortho_out, r_out, coeffs_out, g, ph, pl_, ortho, r, s, t, w, root, sems):
+def factor_kernel(g_in, ph_in, pl_in, coeffs, ortho_out, r_out, coeffs_out, g, ph, pl_, kept, ortho, r, s, t, w, root, sems):
     copies = [pltpu.make_async_copy(a, b, sems.at[i]) for i, (a, b) in enumerate(
-        ((g_in, g), (ph_in, ph), (pl_in, pl_), (coeffs, coeffs_out)))]
+        ((g_in, g), (ph_in, ph), (pl_in, pl_), (coeffs, kept)))]
     for copy in copies:
         copy.start()
     n = 512
@@ -493,9 +493,12 @@
                         s[at, n : n + hi] -= exact(rc, w[lo:hi, 0:hi], TN)
         return carry
 
+    copies[3].wait()
+    stores = [pltpu.make_async_copy(kept, coeffs_out, sems.at[9])]
+    stores[0].start()
     lax.fori_loop(0, 4, body, 0)
-    stores = [pltpu.make_async_copy(r, r_out, sems.at[4])]
-    stores[0].start()
+    stores.append(pltpu.make_async_copy(r, r_out, sems.at[4]))
+    stores[1].start()
     copies[1].wait()
     copies[2].wait()
     wh, wl = split(w[...])
@@ -506,7 +509,6 @@
             ortho[rows, at] = dot3(ph[rows, k], pl_[rows, k], wh[at, k], wl[at, k], NT)
         stores.append(pltpu.make_async_copy(ortho.at[pl.ds(i * 256, 256)], ortho_out.at[pl.ds(i * 256, 256)], sems.at[5 + i]))
         stores[-1].start()
-    copies[3].wait()
     for copy in stores:
         copy.wait()
 
@@ -523,9 +525,9 @@
         out_specs=[anywhere] * 3,
         scratch_shapes=[
             pltpu.VMEM((384, 512), F32), pltpu.VMEM((1024, 512), BF16), pltpu.VMEM((1024, 512), BF16),
-            pltpu.VMEM((1024, 512), F32), pltpu.VMEM((512, 512), F32),
+            pltpu.VMEM((1024, 512), F32), pltpu.VMEM((1024, 512), F32), pltpu.VMEM((512, 512), F32),
             pltpu.VMEM((512, 1024), F32), pltpu.VMEM((128, 256), F32), pltpu.VMEM((512, 512), F32),
-            pltpu.VMEM((8, 512), F32), pltpu.SemaphoreType.DMA((9,)),
+            pltpu.VMEM((8, 512), F32), pltpu.SemaphoreType.DMA((10,)),
         ],
         compiler_params=pltpu.CompilerParams(vmem_limit_bytes=63 * 2**20),
     )(gram, ph, pl_, coeffs)

time: 129 us -> 86.1 us (0.67)
  Pallas kernels: 128 us -> 85.2 us
    pallas_call x1, Pallas kernels: 64.7 us -> 21.9 us  [orthogonalize(): pl.pallas_call(factor_kernel, out_shape=[jax.ShapeDtypeStruct((1024, 512)...]
where the time goes in v3:
time: 86.1 us; the launch traced here: 86 us
  Pallas kernels  85.2 us (99%)
    pallas_call x1, Pallas kernels, project(): pl.pallas_call(functools.partial(project_kernel, 1.0 / rows_total), out_s...  63.3 us
    pallas_call x1, Pallas kernels, orthogonalize(): pl.pallas_call(factor_kernel, out_shape=[jax.ShapeDtypeStruct((1024, 512)...  21.9 us

profile of v3, /device:TPU:1, one launch (start us, length us, event | category | flops | bytes accessed | tf_op | source)
XLA Modules:
  0.0 86.0 jit_solution(14896709489808029738)
XLA Ops:
  0.6 63.3 %shard_map.49 = (bf16[1024,512]{1,0:T(8,128)(2,1)}, bf16[1024,512]{1,0:T(8,128)(2,1)}, f32[384,512]{1,0:T(8,128)}, f32[1024,512]{1,0:T(8,128)}) custom-call(f32[1024,512]{1,0:T(8,128)} %block_in.1, f32[1024,1024]{1,0:T(8,128)} %basis_in.1), custom_call_target="tpu_custom_call" | custom-call | tf_op jit(solution)/shard_map/pallas_call | solution.py:352
  64.0 21.9 %shard_map.50 = (f32[1024,512]{1,0:T(8,128)}, f32[512,512]{1,0:T(8,128)}, f32[1024,512]{1,0:T(8,128)}) custom-call(f32[384,512]{1,0:T(8,128)} %get-tuple-element.7.g_in, bf16[1024,512]{1,0:T(8,128)(2,1)} %get-tuple-element.8.ph_in, bf16[1024,512]{1,0:T(8,128)(2,1)} %get-tuple-element.9.pl_in, f32[1024,512]{1,0:T(8,128)} %get-tuple-element.10.coeffs), custom_call_target="tpu_custom_call" | custom-call | tf_op jit(solution)/shard_map/pallas_call | solution.py:518

commit v4 on v3

--- a/solution.py
+++ b/solution.py
@@ -384,28 +384,23 @@
     def col(v, c):
         return jnp.broadcast_to(v[:, c : c + 1], (8, 128))
 
-    def update(i, lo, zr):
-        a0 = t[8 * i : 8 * i + 8, 0:128]
-        a1 = t[8 * i : 8 * i + 8, 128:256]
-        ci = [col(a0, lo + k) for k in range(8)]
-        s0 = [ci[k] * zr[k][0] for k in range(8)]
-        s1 = [ci[k] * zr[k][1] for k in range(8)]
-        while len(s0) > 1:
-            s0 = [s0[x] + s0[x + 1] for x in range(0, len(s0), 2)]
-            s1 = [s1[x] + s1[x + 1] for x in range(0, len(s1), 2)]
-        v0, v1 = a0 - s0[0], a1 - s1[0]
-        t[8 * i : 8 * i + 8, 0:128] = v0
-        t[8 * i : 8 * i + 8, 128:256] = v1
-        return v0, v1
-
-    v0, v1 = t[0:8, 0:128], t[0:8, 128:256]
-    for p in range(16):
-        lo = 8 * p
-        x = [col(v0, lo + k) for k in range(8)] + [v0, v1]
+    def total(terms):
+        while len(terms) > 1:
+            terms = [terms[i] + terms[i + 1] for i in range(0, len(terms), 2)]
+        return terms[0]
+
+    def stack(v, order):
+        h = v.astype(BF16).astype(F32)
+        m = (v - h).astype(BF16).astype(F32)
+        three = h, m, v - h - m
+        return jnp.concatenate([three[i] for i in order], axis=0).astype(BF16)
+
+    def solve(x, v0, v1, lo):
+        x = x + [v0, v1]
         raw0, raw1 = v0, v1
+        end = len(x)
         a_of = jnp.ones((8, 128), F32)
-        b_of = jnp.zeros((8, 128), F32)
-        d_of = b_of
+        b_of = d_of = jnp.zeros((8, 128), F32)
         for j in range(0, 8, 2):
             even, odd = sub == j, sub == j + 1
             pair = even | odd
@@ -415,24 +410,51 @@
             g = 1.0 / (a * c - b * b)
             n0 = jnp.where(even, c, jnp.where(odd, -b, x[j + 1] * b - x[j] * c))
             n1 = jnp.where(even, -b, jnp.where(odd, a, x[j] * b - x[j + 1] * a))
-            raw0 = jnp.where(even, top[8], jnp.where(odd, low[8], raw0))
-            raw1 = jnp.where(even, top[9], jnp.where(odd, low[9], raw1))
+            raw0 = jnp.where(even, top[end - 2], jnp.where(odd, low[end - 2], raw0))
+            raw1 = jnp.where(even, top[end - 1], jnp.where(odd, low[end - 1], raw1))
             a_of = jnp.where(odd, a, a_of)
             b_of = jnp.where(odd, b, b_of)
             d_of = jnp.where(even, a, jnp.where(odd, c, d_of))
-            for n in range(j + 2, 10):
+            for n in range(j + 2, end):
                 x[n] = jnp.where(pair, 0.0, x[n]) + g * (n0 * top[n] + n1 * low[n])
-        zr = [(row(x[8], k), row(x[9], k)) for k in range(8)]
-        if p < 15:
-            v0, v1 = update(p + 1, lo, zr)
         m = b_of / a_of
         q = 1.0 / jnp.sqrt(d_of - m * b_of)
         u0 = raw0 - m * pltpu.roll(raw0, 1, 0)
         u1 = raw1 - m * pltpu.roll(raw1, 1, 0)
         t[lo : lo + 8, 0:128] = jnp.where(lane >= sub + lo, u0 * q, 0.0)
         t[lo : lo + 8, 128:256] = u1 * q
-        for i in range(p + 2, 16):
-            update(i, lo, zr)
+        return x
+
+    now = [(t[i : i + 8, 0:128], t[i : i + 8, 128:256]) for i in (0, 8)]
+    for p in range(8):
+        lo = 16 * p
+        (a0, a1), (b0, b1) = now
+        own = [col(a0, lo + k) for k in range(8)]
+        across = [col(a0, lo + 8 + k) for k in range(8)]
+        down = [col(b0, lo + k) for k in range(8)]
+        corner = [col(b0, lo + 8 + k) for k in range(8)]
+        x = solve(own + across, a0, a1, lo)
+        across, y0, y1 = x[8:16], x[16], x[17]
+        corner = [corner[k] - total([down[m] * row(across[k], m) for m in range(8)]) for k in range(8)]
+        c0 = b0 - total([down[m] * row(y0, m) for m in range(8)])
+        c1 = b1 - total([down[m] * row(y1, m) for m in range(8)])
+        x = solve(corner, c0, c1, lo + 8)
+        z0, z1 = x[8], x[9]
+        if p == 7:
+            break
+        y0 = y0 - total([across[k] * row(z0, k) for k in range(8)])
+        y1 = y1 - total([across[k] * row(z1, k) for k in range(8)])
+        now = []
+        for i in (lo + 16, lo + 24):
+            v0, v1 = t[i : i + 8, 0:128], t[i : i + 8, 128:256]
+            ci = [col(v0, lo + k) for k in range(16)]
+            now.append((v0 - total([ci[k] * row((y0, z0)[k // 8], k % 8) for k in range(16)]),
+                        v1 - total([ci[k] * row((y1, z1)[k // 8], k % 8) for k in range(16)])))
+        if p < 6:
+            left = stack(jnp.concatenate([a0, b0], axis=0), (0, 0, 1, 0, 2, 1))
+            right = jnp.concatenate([jnp.concatenate([y0, y1], axis=1), jnp.concatenate([z0, z1], axis=1)], axis=0)
+            change = lax.dot_general(left, stack(right, (0, 1, 0, 2, 0, 1)), (((0,), (0,)), ((), ())), preferred_element_type=F32)
+            t[lo + 32 :, :] -= change[lo + 32 :, :]
 
 
 def exact(a, b, dims):
@@ -442,14 +464,15 @@
 def factor_kernel(g_in, ph_in, pl_in, coeffs, ortho_out, r_out, coeffs_out, g, ph, pl_, kept, ortho, r, s, t, w, root, sems):
     copies = [pltpu.make_async_copy(a, b, sems.at[i]) for i, (a, b) in enumerate(
         ((g_in, g), (ph_in, ph), (pl_in, pl_), (coeffs, kept)))]
-    for copy in copies:
-        copy.start()
+    copies[0].start()
     n = 512
     r[...] = jnp.zeros((n, n), F32)
     w[...] = jnp.zeros((n, n), F32)
     s[:, n : 2 * n] = jnp.zeros((n, n), F32)
     eye = lax.broadcasted_iota(jnp.int32, (128, 128), 0) == lax.broadcasted_iota(jnp.int32, (128, 128), 1)
     copies[0].wait()
+    for copy in copies[1:]:
+        copy.start()
     s[0:256, 0:n] = g[0:256, :]
     s[256:384, 256:n] = g[256:384, 0:256]
     s[384:512, 256:n] = g[256:384, 256:n]
@@ -493,10 +516,11 @@
                         s[at, n : n + hi] -= exact(rc, w[lo:hi, 0:hi], TN)
         return carry
 
+    lax.fori_loop(0, 2, body, 0)
     copies[3].wait()
     stores = [pltpu.make_async_copy(kept, coeffs_out, sems.at[9])]
     stores[0].start()
-    lax.fori_loop(0, 4, body, 0)
+    lax.fori_loop(2, 4, body, 0)
     stores.append(pltpu.make_async_copy(r, r_out, sems.at[4]))
     stores[1].start()
     copies[1].wait()

time: 86.1 us -> 82 us (0.952)
  Pallas kernels: 85.2 us -> 81 us
    pallas_call x1, Pallas kernels: 21.9 us -> 17.7 us  [orthogonalize(): pl.pallas_call(factor_kernel, out_shape=[jax.ShapeDtypeStruct((1024, 512)...]
where the time goes in v4:
time: 82 us; the launch traced here: 81.8 us
  Pallas kernels  81 us (99%)
    pallas_call x1, Pallas kernels, project(): pl.pallas_call(functools.partial(project_kernel, 1.0 / rows_total), out_s...  63.3 us
    pallas_call x1, Pallas kernels, orthogonalize(): pl.pallas_call(factor_kernel, out_shape=[jax.ShapeDtypeStruct((1024, 512)...  17.7 us

profile of v4, /device:TPU:1, one launch (start us, length us, event | category | flops | bytes accessed | tf_op | source)
XLA Modules:
  0.0 81.8 jit_solution(13922004728932106212)
XLA Ops:
  0.6 63.3 %shard_map.49 = (bf16[1024,512]{1,0:T(8,128)(2,1)}, bf16[1024,512]{1,0:T(8,128)(2,1)}, f32[384,512]{1,0:T(8,128)}, f32[1024,512]{1,0:T(8,128)}) custom-call(f32[1024,512]{1,0:T(8,128)} %block_in.1, f32[1024,1024]{1,0:T(8,128)} %basis_in.1), custom_call_target="tpu_custom_call" | custom-call | tf_op jit(solution)/shard_map/pallas_call | solution.py:352
  64.0 17.7 %shard_map.50 = (f32[1024,512]{1,0:T(8,128)}, f32[512,512]{1,0:T(8,128)}, f32[1024,512]{1,0:T(8,128)}) custom-call(f32[384,512]{1,0:T(8,128)} %get-tuple-element.7.g_in, bf16[1024,512]{1,0:T(8,128)(2,1)} %get-tuple-element.8.ph_in, bf16[1024,512]{1,0:T(8,128)(2,1)} %get-tuple-element.9.pl_in, f32[1024,512]{1,0:T(8,128)} %get-tuple-element.10.coeffs), custom_call_target="tpu_custom_call" | custom-call | tf_op jit(solution)/shard_map/pallas_call | solution.py:542

commit v5 on v4

--- a/solution.py
+++ b/solution.py
@@ -9,7 +9,6 @@
 F32 = jnp.float32
 BF16 = jnp.bfloat16
 MESH = pl.DeviceIdType.MESH
-HI = lax.Precision.HIGHEST
 AXES = ((0, 1, 2), (1, 2, 0), (2, 0, 1))
 
 
@@ -370,7 +369,7 @@
             pltpu.SemaphoreType.DMA((3,)),
         ],
         compiler_params=pltpu.CompilerParams(
-            collective_id=0, has_side_effects=True, vmem_limit_bytes=60 * 2**20),
+            collective_id=0, has_side_effects=True, vmem_limit_bytes=48 * 2**20),
     )(block, basis)
 
 
@@ -457,22 +456,24 @@
             t[lo + 32 :, :] -= change[lo + 32 :, :]
 
 
-def exact(a, b, dims):
-    return lax.dot_general(a, b, (dims, ((), ())), precision=HI, preferred_element_type=F32)
-
-
-def factor_kernel(g_in, ph_in, pl_in, coeffs, ortho_out, r_out, coeffs_out, g, ph, pl_, kept, ortho, r, s, t, w, root, sems):
-    copies = [pltpu.make_async_copy(a, b, sems.at[i]) for i, (a, b) in enumerate(
-        ((g_in, g), (ph_in, ph), (pl_in, pl_), (coeffs, kept)))]
-    copies[0].start()
+SECOND = (0, 1, 0, 2, 0, 1)
+
+
+def parts(v, order, axis):
+    h = v.astype(BF16).astype(F32)
+    m = (v - h).astype(BF16).astype(F32)
+    three = [each.astype(BF16) for each in (h, m, v - h - m)]
+    return jnp.concatenate([three[i] for i in order], axis=axis)
+
+
+def factor_kernel(g, ph, pl_, coeffs, ortho_out, r_out, coeffs_out, ortho, r, s, t, w, root, sems):
+    stores = [pltpu.make_async_copy(coeffs, coeffs_out, sems.at[0])]
+    stores[0].start()
     n = 512
     r[...] = jnp.zeros((n, n), F32)
     w[...] = jnp.zeros((n, n), F32)
     s[:, n : 2 * n] = jnp.zeros((n, n), F32)
     eye = lax.broadcasted_iota(jnp.int32, (128, 128), 0) == lax.broadcasted_iota(jnp.int32, (128, 128), 1)
-    copies[0].wait()
-    for copy in copies[1:]:
-        copy.start()
     s[0:256, 0:n] = g[0:256, :]
     s[256:384, 256:n] = g[256:384, 0:256]
     s[384:512, 256:n] = g[256:384, 256:n]
@@ -504,34 +505,33 @@
                 li = scaled * root[0:1, lo:hi]
                 r[lo:hi, lo:hi] = t[:, 0:128] * root[0:1, lo:hi]
                 w[lo:hi, lo:hi] = scaled
+                left = parts(li, (0, 0, 1, 0, 2, 1), 1)
                 if b:
-                    w[lo:hi, 0:lo] = exact(li, s[lo:hi, n : n + lo], NN)
+                    w[lo:hi, 0:lo] = dot(left, parts(s[lo:hi, n : n + lo], SECOND, 0), NN)
                 if b < 3:
-                    right = exact(li, s[lo:hi, hi:n], NN)
+                    right = dot(left, parts(s[lo:hi, hi:n], SECOND, 0), NN)
                     r[lo:hi, hi:n] = right * root[0:1, hi:n]
+                    down = parts(right, (0, 0, 1, 0, 2, 1), 0)
+                    across = parts(right, SECOND, 0)
+                    inverse = parts(w[lo:hi, 0:hi], SECOND, 0)
                     for c in range(b + 1, 4):
                         at = slice(c * 128, c * 128 + 128)
-                        rc = right[:, (c - b - 1) * 128 : (c - b) * 128]
-                        s[at, c * 128 : n] -= exact(rc, right[:, (c - b - 1) * 128 :], TN)
-                        s[at, n : n + hi] -= exact(rc, w[lo:hi, 0:hi], TN)
+                        first = (c - b - 1) * 128
+                        rows = down[:, first : first + 128]
+                        s[at, c * 128 : n] -= dot(rows, across[:, first:], TN)
+                        s[at, n : n + hi] -= dot(rows, inverse, TN)
         return carry
 
-    lax.fori_loop(0, 2, body, 0)
-    copies[3].wait()
-    stores = [pltpu.make_async_copy(kept, coeffs_out, sems.at[9])]
-    stores[0].start()
-    lax.fori_loop(2, 4, body, 0)
-    stores.append(pltpu.make_async_copy(r, r_out, sems.at[4]))
+    lax.fori_loop(0, 4, body, 0)
+    stores.append(pltpu.make_async_copy(r, r_out, sems.at[1]))
     stores[1].start()
-    copies[1].wait()
-    copies[2].wait()
     wh, wl = split(w[...])
     for i in range(4):
         rows = slice(i * 256, i * 256 + 256)
         for c in range(2):
             at, k = slice(c * 256, c * 256 + 256), slice(0, c * 256 + 256)
             ortho[rows, at] = dot3(ph[rows, k], pl_[rows, k], wh[at, k], wl[at, k], NT)
-        stores.append(pltpu.make_async_copy(ortho.at[pl.ds(i * 256, 256)], ortho_out.at[pl.ds(i * 256, 256)], sems.at[5 + i]))
+        stores.append(pltpu.make_async_copy(ortho.at[pl.ds(i * 256, 256)], ortho_out.at[pl.ds(i * 256, 256)], sems.at[2 + i]))
         stores[-1].start()
     for copy in stores:
         copy.wait()
@@ -545,15 +545,14 @@
             jax.ShapeDtypeStruct((1024, 512), F32), jax.ShapeDtypeStruct((512, 512), F32),
             jax.ShapeDtypeStruct((1024, 512), F32),
         ],
-        in_specs=[anywhere] * 4,
+        in_specs=[pl.BlockSpec(memory_space=pltpu.VMEM)] * 3 + [anywhere],
         out_specs=[anywhere] * 3,
         scratch_shapes=[
-            pltpu.VMEM((384, 512), F32), pltpu.VMEM((1024, 512), BF16), pltpu.VMEM((1024, 512), BF16),
-            pltpu.VMEM((1024, 512), F32), pltpu.VMEM((1024, 512), F32), pltpu.VMEM((512, 512), F32),
+            pltpu.VMEM((1024, 512), F32), pltpu.VMEM((512, 512), F32),
             pltpu.VMEM((512, 1024), F32), pltpu.VMEM((128, 256), F32), pltpu.VMEM((512, 512), F32),
-            pltpu.VMEM((8, 512), F32), pltpu.SemaphoreType.DMA((10,)),
+            pltpu.VMEM((8, 512), F32), pltpu.SemaphoreType.DMA((6,)),
         ],
-        compiler_params=pltpu.CompilerParams(vmem_limit_bytes=63 * 2**20),
+        compiler_params=pltpu.CompilerParams(vmem_limit_bytes=40 * 2**20),
     )(gram, ph, pl_, coeffs)
 
 

time: 82 us -> 79.6 us (0.971)
  Pallas kernels: 81 us -> 78.7 us
    pallas_call x1, Pallas kernels: 17.7 us -> 16 us  [orthogonalize(): pl.pallas_call(factor_kernel, out_shape=[jax.ShapeDtypeStruct((1024, 512)...]
where the time goes in v5:
time: 79.6 us; the launch traced here: 79.5 us
  Pallas kernels  78.7 us (99%)
  between operations  0.8 us (1%)
    pallas_call x1, Pallas kernels, project(): pl.pallas_call(functools.partial(project_kernel, 1.0 / rows_total), out_s...  62.7 us
    pallas_call x1, Pallas kernels, orthogonalize(): pl.pallas_call(factor_kernel, out_shape=[jax.ShapeDtypeStruct((1024, 512)...  16 us

profile of v5, /device:TPU:1, one launch (start us, length us, event | category | flops | bytes accessed | tf_op | source)
XLA Modules:
  0.0 79.5 jit_solution(11323641145005701930)
XLA Ops:
  0.6 62.7 %shard_map.49 = (bf16[1024,512]{1,0:T(8,128)(2,1)S(1)}, bf16[1024,512]{1,0:T(8,128)(2,1)S(1)}, f32[384,512]{1,0:T(8,128)S(1)}, f32[1024,512]{1,0:T(8,128)S(1)}) custom-call(f32[1024,512]{1,0:T(8,128)} %block_in.1, f32[1024,1024]{1,0:T(8,128)} %basis_in.1), custom_call_target="tpu_custom_call" | custom-call | tf_op jit(solution)/shard_map/pallas_call | solution.py:351
  63.4 16.0 %shard_map.50 = (f32[1024,512]{1,0:T(8,128)}, f32[512,512]{1,0:T(8,128)}, f32[1024,512]{1,0:T(8,128)}) custom-call(f32[384,512]{1,0:T(8,128)S(1)} %get-tuple-element.7.g, bf16[1024,512]{1,0:T(8,128)(2,1)S(1)} %get-tuple-element.8.ph, bf16[1024,512]{1,0:T(8,128)(2,1)S(1)} %get-tuple-element.9.pl_, f32[1024,512]{1,0:T(8,128)S(1)} %get-tuple-element.10.coeffs), custom_call_target="tpu_custom_call" | custom-call | tf_op jit(solution)/shard_map/pallas_call | solution.py:542

commit v6 on v5

--- a/solution.py
+++ b/solution.py
@@ -282,7 +282,7 @@
             for s in range(3):
                 getattr(each, phase)(s)
 
-    def subtract(at):
+    def subtract(at, last=False):
         rows = pl.ds(pl.multiple_of(at, 256), 256)
         hi, lo = split(coeffs[rows, :])
         kh[rows, :] = hi
@@ -291,7 +291,13 @@
         @pl.loop(0, 4)
         def _(i):
             at = pl.ds(pl.multiple_of(i * 256, 256), 256)
-            bk[at, :] -= dot3(sh[at, rows], sl[at, rows], kh[rows, :], kl[rows, :], NN)
+            left = bk[at, :] - dot3(sh[at, rows], sl[at, rows], kh[rows, :], kl[rows, :], NN)
+            if last:
+                hi, lo = split(left)
+                ph[at, :] = hi
+                pl_[at, :] = lo
+            else:
+                bk[at, :] = left
 
     for i in range(2):
         for ks in ((1, 3), (2,)):
@@ -300,17 +306,10 @@
         subtract(core * 512 + i * 256)
     for i in range(2):
         sums[i].meet()
-        subtract((1 - core) * 512 + i * 256)
+        subtract((1 - core) * 512 + i * 256, last=i == 1)
 
     keep = [pltpu.make_async_copy(coeffs, coeffs_out, store.at[0])]
     keep[0].start()
-
-    @pl.loop(0, 4)
-    def _(i):
-        at = pl.ds(pl.multiple_of(i * 256, 256), 256)
-        hi, lo = split(bk[at, :])
-        ph[at, :] = hi
-        pl_[at, :] = lo
 
     keep += [pltpu.make_async_copy(ph, ph_out, store.at[1]), pltpu.make_async_copy(pl_, pl_out, store.at[2])]
     keep[1].start()
@@ -470,9 +469,14 @@
     stores = [pltpu.make_async_copy(coeffs, coeffs_out, sems.at[0])]
     stores[0].start()
     n = 512
-    r[...] = jnp.zeros((n, n), F32)
-    w[...] = jnp.zeros((n, n), F32)
-    s[:, n : 2 * n] = jnp.zeros((n, n), F32)
+    zeros = jnp.zeros((128, 128), F32)
+    for b in range(4):
+        at = slice(b * 128, b * 128 + 128)
+        for c in range(b):
+            r[at, c * 128 : c * 128 + 128] = zeros
+            s[at, n + c * 128 : n + c * 128 + 128] = zeros
+        if b % 2 == 0:
+            w[at, b * 128 + 128 : b * 128 + 256] = zeros
     eye = lax.broadcasted_iota(jnp.int32, (128, 128), 0) == lax.broadcasted_iota(jnp.int32, (128, 128), 1)
     s[0:256, 0:n] = g[0:256, :]
     s[256:384, 256:n] = g[256:384, 0:256]
@@ -525,12 +529,12 @@
     lax.fori_loop(0, 4, body, 0)
     stores.append(pltpu.make_async_copy(r, r_out, sems.at[1]))
     stores[1].start()
-    wh, wl = split(w[...])
+    halves = [split(w[c * 256 : c * 256 + 256, 0 : c * 256 + 256]) for c in range(2)]
     for i in range(4):
         rows = slice(i * 256, i * 256 + 256)
         for c in range(2):
             at, k = slice(c * 256, c * 256 + 256), slice(0, c * 256 + 256)
-            ortho[rows, at] = dot3(ph[rows, k], pl_[rows, k], wh[at, k], wl[at, k], NT)
+            ortho[rows, at] = dot3(ph[rows, k], pl_[rows, k], *halves[c], NT)
         stores.append(pltpu.make_async_copy(ortho.at[pl.ds(i * 256, 256)], ortho_out.at[pl.ds(i * 256, 256)], sems.at[2 + i]))
         stores[-1].start()
     for copy in stores:

time: 79.6 us -> 79.2 us (level)
  no operation moved by 1% of the time
where the time goes in v6:
time: 79.2 us; the launch traced here: 79.1 us
  Pallas kernels  78.3 us (99%)
  between operations  0.8 us (1%)
    pallas_call x1, Pallas kernels, project(): pl.pallas_call(functools.partial(project_kernel, 1.0 / rows_total), out_s...  62.4 us
    pallas_call x1, Pallas kernels, orthogonalize(): pl.pallas_call(factor_kernel, out_shape=[jax.ShapeDtypeStruct((1024, 512)...  15.9 us

profile of v6, /device:TPU:1, one launch (start us, length us, event | category | flops | bytes accessed | tf_op | source)
XLA Modules:
  0.0 79.1 jit_solution(6504762776769464330)
XLA Ops:
  0.6 62.4 %shard_map.49 = (bf16[1024,512]{1,0:T(8,128)(2,1)S(1)}, bf16[1024,512]{1,0:T(8,128)(2,1)S(1)}, f32[384,512]{1,0:T(8,128)S(1)}, f32[1024,512]{1,0:T(8,128)S(1)}) custom-call(f32[1024,512]{1,0:T(8,128)} %block_in.1, f32[1024,1024]{1,0:T(8,128)} %basis_in.1), custom_call_target="tpu_custom_call" | custom-call | tf_op jit(solution)/shard_map/pallas_call | solution.py:350
  63.1 15.9 %shard_map.50 = (f32[1024,512]{1,0:T(8,128)}, f32[512,512]{1,0:T(8,128)}, f32[1024,512]{1,0:T(8,128)}) custom-call(f32[384,512]{1,0:T(8,128)S(1)} %get-tuple-element.7.g, bf16[1024,512]{1,0:T(8,128)(2,1)S(1)} %get-tuple-element.8.ph, bf16[1024,512]{1,0:T(8,128)(2,1)S(1)} %get-tuple-element.9.pl_, f32[1024,512]{1,0:T(8,128)S(1)} %get-tuple-element.10.coeffs), custom_call_target="tpu_custom_call" | custom-call | tf_op jit(solution)/shard_map/pallas_call | solution.py:546
